TPU v7x, 32 devices: a whole 2x2x4 slice. The times are simulated.
32 devices in a mesh: role: 2 (over y), tile: 16 (over z, x, core).
Axes of the slice: x: 2, y: 2, z: 4, core: 2. Of those that a mesh axis runs over, the one named last changes fastest.
Arguments:
- fields_pair: float32 [2, 512, 16384], P('role', None, 'tile'), may hold values from 0 to 1
- velocity: float32 [16384], P('tile'), may hold values from -0.5 to 0.5
- growth: float32 [16384], P('tile'), may hold values from 0.05 to 0.5
- features: bfloat16 [512, 1024], replicated, may hold values from -6 to 6
- assignment: int32 [512], replicated, may hold values from 0 to 511, each once
- out_pair: float32 [2, 1024, 16384], P('role', None, 'tile'), may hold values from -0.1875 to 0.1875
- hidden_pair: float32 [2, 5, 1024, 1024], P('role', None, 'tile'), may hold values from -0.1875 to 0.1875
Outputs:
- fields_next: float32 [2, 512, 16384], P('role', None, 'tile')
- out_next: float32 [2, 1024, 16384], P('role', None, 'tile')
- hidden_next: float32 [2, 5, 1024, 1024], P('role', None, 'tile')
Inputs may be any that keep to these rules, and one draw needn't show every extreme that they name: `assignment`: a permutation of the 512 members.
All inputs are finite; a program needn't handle non-finite values.
Results may differ from a plain program's by a relative error of at most 0.0022.
The roundings to bfloat16 on the way count: a program that leaves them out, or rounds other values in their place, can miss the bound.
Values may be sent and summed in bfloat16 or wider, within the bound.
A program may use at most 192 MiB of HBM per device.

v0:
```python
import jax
import jax.numpy as jnp
from jax import lax
from jax.sharding import PartitionSpec as P

BATCH = 512
momentum_decay = 0.9
step_size = 0.1


def extended(value, sides, width):
    for axis, dim in sides:
        count, length = (lax.axis_size(axis), value.shape[dim])
        up = [(i, (i + 1) % count) for i in range(count)]
        down = [(j, i) for i, j in up]
        last = lax.slice_in_dim(value, length - width, length, axis=dim)
        leading = lax.slice_in_dim(value, 0, width, axis=dim)
        before = lax.ppermute(last, axis, up)
        after = lax.ppermute(leading, axis, down)
        value = jnp.concatenate([before, value, after], axis=dim)
    return value


def spread(block, axis, owner):
    block = jnp.where(lax.axis_index(axis) == owner, block, jnp.zeros_like(block))
    return lax.psum(block, axis)


def partner(value, axis, distance):
    return lax.ppermute(value, axis, [(i, i ^ 1 << distance) for i in range(lax.axis_size(axis))])


def guarded(flag, action, *operands):

    def skipped(*values):
        return jax.tree.map(jnp.zeros_like, action(*values))

    return lax.cond(flag, action, skipped, *operands)


def silu_slope(values):
    logistic = jax.nn.sigmoid(values)
    return logistic * (1.0 + values * (1.0 - logistic))


def advance(padded, growth):
    states = padded[:-1]
    velocity_row = padded[-1]
    outflow = (
        jnp.maximum(velocity_row[:-1], 0.0) * states[:, :-1]
        + jnp.minimum(velocity_row[:-1], 0.0) * states[:, 1:]
    )
    carried = states[:, 1:-1] - outflow[:, 1:] + outflow[:, :-1]
    return carried + growth * carried * (1.0 - carried)


def body(fields_pair, velocity, growth, features, assignment, out_pair, hidden_pair):
    solver_side = lax.axis_index("role") == 0
    trainer_side = jnp.logical_not(solver_side)
    own_fields = fields_pair[0]
    own_out = out_pair[0]
    own_hidden = hidden_pair[0]
    layer_count = own_hidden.shape[0]
    unit_rows = own_hidden.shape[1]
    first_unit = lax.axis_index("tile") * unit_rows
    stacked = jnp.concatenate([own_fields, velocity[None, :]], axis=0)
    padded = extended(stacked, (("tile", 1),), 1)
    advanced = guarded(solver_side, advance, padded, growth)
    fresh_fields = spread(advanced, "role", 0)
    out_narrow = own_out.astype(jnp.bfloat16)
    hidden_narrow = own_hidden.astype(jnp.bfloat16)
    full_hidden = lax.all_gather(hidden_narrow, "tile", axis=1, tiled=True)

    def forward(features, full_hidden, out_narrow, target):
        inputs = []
        summed_list = []
        activation = features
        for layer_index in range(layer_count):
            inputs.append(activation)
            summed = jnp.dot(
                activation, full_hidden[layer_index], preferred_element_type=jnp.float32
            )
            summed_list.append(summed)
            activation = jax.nn.silu(summed).astype(jnp.bfloat16)
        predicted = jnp.dot(activation, out_narrow, preferred_element_type=jnp.float32)
        residual = ((predicted - target) / BATCH).astype(jnp.bfloat16)
        grad_out = jnp.dot(activation.T, residual, preferred_element_type=jnp.float32)
        partial_grad = lax.dot_general(
            residual, out_narrow, (((1,), (1,)), ((), ())), preferred_element_type=jnp.float32
        )
        return (jnp.stack(summed_list), jnp.stack(inputs), grad_out, partial_grad)

    summed_all, inputs_all, grad_out, partial_grad = guarded(
        trainer_side, forward, features, full_hidden, out_narrow, own_fields
    )
    upstream = lax.psum(partial_grad, "tile")

    def backward(summed_all, inputs_all, upstream, full_hidden, first_unit):
        gradients = []
        for layer_index in reversed(range(layer_count)):
            slope = (upstream * silu_slope(summed_all[layer_index])).astype(jnp.bfloat16)
            own_inputs = lax.dynamic_slice_in_dim(inputs_all[layer_index], first_unit, unit_rows, 1)
            gradients.append(jnp.dot(own_inputs.T, slope, preferred_element_type=jnp.float32))
            if layer_index > 0:
                upstream = lax.dot_general(
                    slope,
                    full_hidden[layer_index],
                    (((1,), (1,)), ((), ())),
                    preferred_element_type=jnp.float32,
                )
        return jnp.stack(gradients[::-1])

    grad_hidden = guarded(
        trainer_side, backward, summed_all, inputs_all, upstream, full_hidden, first_unit
    )
    solver_pack = jnp.concatenate([own_out.reshape(-1), own_hidden.reshape(-1)])
    trainer_pack = jnp.concatenate([grad_out.reshape(-1), grad_hidden.reshape(-1)])
    payload = jnp.where(solver_side, solver_pack, trainer_pack)
    received = partner(payload, "role", 0)
    out_length = own_out.size
    other_out = received[:out_length].reshape(own_out.shape)
    other_hidden = received[out_length:].reshape(own_hidden.shape)
    out_next = jnp.where(
        solver_side,
        momentum_decay * own_out + other_out,
        own_out - step_size * (momentum_decay * other_out + grad_out),
    )
    hidden_next = jnp.where(
        solver_side,
        momentum_decay * own_hidden + other_hidden,
        own_hidden - step_size * (momentum_decay * other_hidden + grad_hidden),
    )
    fields_next = jnp.where(solver_side, advanced, jnp.take(fresh_fields, assignment, axis=0))
    return (fields_next[None], out_next[None], hidden_next[None])


def solution(mesh):
    return jax.shard_map(
        body,
        mesh=mesh,
        in_specs=(
            P("role", None, "tile"),
            P("tile"),
            P("tile"),
            P(),
            P(),
            P("role", None, "tile"),
            P("role", None, "tile", None),
        ),
        out_specs=(P("role", None, "tile"), P("role", None, "tile"), P("role", None, "tile", None)),
        check_vma=False,
    )
```

profile of v0, /device:TPU:0, one launch (start us, length us, event | category | flops | bytes accessed | tf_op | source)
XLA Modules:
  0.0 473.0 jit_solution(12022284242264037515)
XLA Ops:
  8.1 2.4 bitcast_convert_fusion
  10.5 91.3 %all-gather.2.cloned.1.call-done = bf16[5,1024,1024]{2,1,0:T(8,128)(2,1)} async-done(((bf16[5,64,1024]{2,1,0:T(8,128)(2,1)}), bf16[5,1024,1024]{2,1,0:T(8,128)(2,1)}) %all-gather.2.cloned.1.call-update) | async-done | bytes 10485776 | tf_op jit(solution)/shard_map/all_gather | solution.py:72
  101.9 14.5 %conditional.4 = (f32[5,512,1024]{2,1,0:T(8,128)}, bf16[5,512,1024]{2,1,0:T(8,128)(2,1)}, f32[1024,1024]{1,0:T(8,128)}, f32[512,1024]{1,0:T(8,128)}, f32[1048576]{0:T(1024)}) conditional(s32[]{:T(128)} %convert_element_type.53, () %tuple.39, (bf16[5,1024,1024]{2,1,0:T(8,128)(2,1)}, bf16[512,1024]{1,0:T(8,128)(2,1)}, f32[1024,1024]{1,0:T(8,128)}, ...), branch_computations={%region_3.4_spmd, %region_4.5_spmd} | conditional | flops 8619819008 | bytes 140509344 | solution.py:38
  101.9 5.2 %broadcast.47 = f32[5,512,1024]{2,1,0:T(8,128)} broadcast(f32[]{:T(128)} %constant.41.clone), dimensions={} | broadcast | bytes 10485764 | tf_op jit(solution)/shard_map/broadcast.16
  107.1 3.0 broadcast.48
  110.1 2.5 broadcast.49
  112.6 2.2 reshape.52
  114.8 1.6 broadcast.50
  116.5 5.4 %copy.14 = f32[128,8,8,128]{3,1,2,0:T(8,128)} copy(f32[128,8,8,128]{3,2,1,0:T(8,128)} %bitcast.240) | data formatting | bytes 8388608
  122.2 113.0 %all-reduce.5.cloned.1.call-done = f32[512,1024]{1,0:T(8,128)} async-done(((f32[512,1024]{1,0:T(8,128)}), f32[512,1024]{1,0:T(8,128)}) %all-reduce.5.cloned.1.call-update) | async-done | bytes 2097168 | tf_op jit(solution)/shard_map/psum | solution.py:96
  235.2 2.4 conditional.5
  235.2 1.2 broadcast.52
  236.4 1.1 reshape.54
  237.5 6.3 %maximum_select_fusion = f32[1376256]{0:T(1024)} fusion(f32[327680]{0:T(1024)S(1)} %bitcast.246, f32[1048576]{0:T(1024)} %bitcast.241, f32[327680]{0:T(1024)} %get-tuple-element.66, f32[1048576]{0:T(1024)} %get-tuple-element.62, pred[]{:T(512)S(6)} %eq.4), kind=kLoop, calls=%fused_computation.125 | loop fusion | flops 4128768 | bytes 16515073 | tf_op jit(solution)/shard_map/jit(_where)/select_n | solution.py:118
  243.9 37.5 %collective-permute-start.2 = (f32[1376256]{0:T(1024)}, f32[1376256]{0:T(1024)}, u32[]{:S(2)}, u32[]{:S(2)}) collective-permute-start(f32[1376256]{0:T(1024)} %maximum_select_fusion), channel_id=1, source_target_pairs={{0,16},{16,0},{1,17},{17,1},{2,18},{18,2},{3,19},{19,3},{4,20},{20... | collective-permute-start | bytes 16515080 | tf_op jit(solution)/shard_map/ppermute | solution.py:30
  281.6 4.4 collective-permute-start.1
  286.0 1.6 pad_maximum_fusion
  287.6 2.6 collective-permute-done
  290.2 3.1 concatenate.13
  293.3 3.4 conditional.3
  293.6 0.7 multiply_add_fusion
  294.3 2.5 multiply_add_fusion.1
  296.8 3.2 broadcast_select_fusion
  300.7 107.6 %all-reduce.3.cloned.1.call-done = f32[512,1024]{1,0:T(8,128)} async-done(((f32[512,1024]{1,0:T(8,128)}), f32[512,1024]{1,0:T(8,128)}) %all-reduce.3.cloned.1.call-update) | async-done | bytes 2097168 | tf_op jit(solution)/shard_map/psum | solution.py:26
  408.2 4.4 gather_fusion
  412.6 3.2 select_bitcast_fusion.1
  415.8 28.6 %collective-permute-done.2 = f32[1376256]{0:T(1024)} collective-permute-done((f32[1376256]{0:T(1024)}, f32[1376256]{0:T(1024)}, u32[]{:S(2)}, u32[]{:S(2)}) %collective-permute-start.2) | collective-permute-done | bytes 5505056 | tf_op jit(solution)/shard_map/ppermute | solution.py:30
  444.4 1.4 slice.144
  446.1 4.4 slice.143
  450.5 5.1 %slice.132 = f32[1024,1024]{1,0:T(8,128)} reshape(f32[1048576]{0:T(1024)} %slice.143) | data formatting | bytes 8388608 | tf_op jit(solution)/shard_map/slice | solution.py:121
  455.6 3.0 fusion.100
  458.6 7.1 %select_bitcast_fusion = f32[1,1024,1024]{2,1,0:T(8,128)} fusion(f32[1024,1024]{1,0:T(8,128)} %get-tuple-element.67, f32[1024,1024]{1,0:T(8,128)} %slice.132, pred[]{:T(512)S(6)} %eq.4, f32[1,1024,1024]{2,1,0:T(8,128)S(1)} %copy-done), kind=kLoop, calls=%fused_computation.126 | loop fusion | flops 7340032 | bytes 16777216 | tf_op jit(solution)/shard_map/broadcast_in_dim | solution.py:134
  (29 shorter events, 1.6 us)
Async XLA Ops:
  8.0 93.9 %copy-start.4 = (f32[1,512,1024]{2,1,0:T(8,128)S(1)}, f32[1,512,1024]{2,1,0:T(8,128)}, u32[]{:S(2)}) copy-start(f32[1,512,1024]{2,1,0:T(8,128)} %param.13) | copy-start | bytes 6291460
  8.0 93.9 %all-gather.2.cloned.1.call-start = ((), (), s32[]{:S(2)}) async-start(), calls=%async_computation.1 | async-start | bytes 11141120 | tf_op jit(solution)/shard_map/all_gather | solution.py:72
  10.5 224.7 %all-reduce.5.cloned.1.call-start = ((), (), s32[]{:S(2)}) async-start(), calls=%async_computation.2 | async-start | bytes 4194304 | tf_op jit(solution)/shard_map/psum | solution.py:96
  116.4 291.8 %all-reduce.3.cloned.1.call-start = ((), (), s32[]{:S(2)}) async-start(), calls=%async_computation | async-start | bytes 4194304 | tf_op jit(solution)/shard_map/psum | solution.py:26
  116.5 5.4 %copy-start.2 = (f32[1,5,64,1024]{3,2,1,0:T(8,128)S(1)}, f32[1,5,64,1024]{3,2,1,0:T(8,128)}, u32[]{:S(2)}) copy-start(f32[1,5,64,1024]{3,2,1,0:T(8,128)} %param.19) | copy-start | bytes 3932164
  237.5 43.8 %copy-start.11 = (f32[1024]{0:T(1024)S(1)}, f32[1024]{0:T(1024)}, u32[]{:S(2)}) copy-start(f32[1024]{0:T(1024)} %param.14) | copy-start | bytes 12292
  243.9 200.6 %collective-permute-start.2 = (f32[1376256]{0:T(1024)}, f32[1376256]{0:T(1024)}, u32[]{:S(2)}, u32[]{:S(2)}) collective-permute-start(f32[1376256]{0:T(1024)} %maximum_select_fusion), channel_id=1, source_target_pairs={{0,16},{16,0},{1,17},{17,1},{2,18},{18,2},{3,19},{19,3},{4,20},{20... | collective-permute-start | bytes 16515080 | tf_op jit(solution)/shard_map/ppermute | solution.py:30
  281.5 8.7 %collective-permute-start = (f32[513,1]{1,0:T(8,128)S(1)}, f32[513,1]{1,0:T(8,128)S(1)}, u32[]{:S(2)}, u32[]{:S(2)}) collective-permute-start(f32[513,1]{1,0:T(8,128)S(1)} %get-tuple-element.91), channel_id=1, source_target_pairs={{0,1},{1,2},{2,3},{3,4},{4,5},{5,6},{6,7},{7,8},{8,9},{9,10},{10,1... | collective-permute-start | bytes 6164 | tf_op jit(solution)/shard_map/ppermute | solution.py:18
  281.6 8.6 %collective-permute-start.1 = (f32[513,1]{1,0:T(8,128)S(1)}, f32[513,1]{1,0:T(8,128)S(1)}, u32[]{:S(2)}, u32[]{:S(2)}) collective-permute-start(f32[513,1]{1,0:T(8,128)S(1)} %get-tuple-element.90), channel_id=1, source_target_pairs={{1,0},{2,1},{3,2},{4,3},{5,4},{6,5},{7,6},{8,7},{9,8},{10,9},{11,1... | collective-permute-start | bytes 6164 | tf_op jit(solution)/shard_map/ppermute | solution.py:19
  287.6 5.7 %copy-start.13 = (f32[1024]{0:T(1024)S(1)}, f32[1024]{0:T(1024)}, u32[]{:S(2)}) copy-start(f32[1024]{0:T(1024)} %param.15) | copy-start | bytes 12292
  300.0 0.7 copy-start.12
  450.5 5.1 %copy-start.3 = (f32[1,5,64,1024]{3,2,1,0:T(8,128)S(1)}, f32[1,5,64,1024]{3,2,1,0:T(8,128)}, u32[]{:S(2)}) copy-start(f32[1,5,64,1024]{3,2,1,0:T(8,128)} %param.19) | copy-start | bytes 3932164
  455.6 3.0 copy-start
Sparse Core Ops, SparseCore 0:
  11.6 90.2 all-gather.1
  116.6 118.5 all-reduce.4
Sparse Core Ops, SparseCore 1:
  300.1 108.1 all-reduce.2
where the time goes:
time: 473 us
  waiting for transfers between devices  343 us (73%)
  starting transfers between devices  42.1 us (9%)
  local copies, waits for them, and re-layouts  41.8 us (9%)
  other arithmetic  30.1 us (6%)
  between operations  15.6 us (3%)
    psum x1, waiting for transfers between devices, body(): upstream = lax.psum(partial_grad, 'tile')  113 us
    psum x1, waiting for transfers between devices, spread(): return lax.psum(block, axis)  108 us
    all_gather x1, waiting for transfers between devices, body(): full_hidden = lax.all_gather(hidden_narrow, 'tile', axis=1, tiled=True)  91.3 us
    ppermute x1, starting transfers between devices, partner(): lax.ppermute(value, axis, [(i, i ^ 1 << distance) for i in range(lax.axis...  37.5 us
    ppermute x1, waiting for transfers between devices, partner(): lax.ppermute(value, axis, [(i, i ^ 1 << distance) for i in range(lax.axis...  28.6 us
    another operation x5, local copies, waits for them, and re-layouts  13.6 us
    broadcast_in_dim x3, other arithmetic, body(): return (fields_next[None], out_next[None], hidden_next[None])  13.2 us
    slice x2, local copies, waits for them, and re-layouts, body(): other_out = received[:out_length].reshape(own_out.shape)  9.5 us
  transfers between devices with their start and end apart: 6, of which 5 were waited for; matrix products, arithmetic and copies ran while one was open for 5% of the time, Pallas kernels for 0%

commit v1 on v0

--- a/solution.py
+++ b/solution.py
@@ -93,7 +93,11 @@
     summed_all, inputs_all, grad_out, partial_grad = guarded(
         trainer_side, forward, features, full_hidden, out_narrow, own_fields
     )
-    upstream = lax.psum(partial_grad, "tile")
+    upstream = partial_grad
+    for hop in (1, 2, 4, 8):
+        upstream = upstream + lax.ppermute(
+            upstream, "tile", [(dev, dev ^ hop) for dev in range(16)]
+        )
 
     def backward(summed_all, inputs_all, upstream, full_hidden, first_unit):
         gradients = []

time: 473 us -> 563 us (1.19)
  waiting for transfers between devices: 343 us -> 413 us
  starting transfers between devices: 42.1 us -> 66.8 us
  local copies, waits for them, and re-layouts: 41.8 us -> 34.6 us
    ppermute x0 -> x4, waiting for transfers between devices: none -> 182 us  [body(): lax.ppermute(upstream, 'tile', [(dev, dev ^ hop) for dev in range(16)])]
    psum x1 -> x0, waiting for transfers between devices: 113 us -> none  [body(): upstream = lax.psum(partial_grad, 'tile')]
    ppermute x1, starting transfers between devices: 37.5 us -> 58.9 us  [partner(): lax.ppermute(value, axis, [(i, i ^ 1 << distance) for i in range(lax.axis...]
  transfers between devices with their start and end apart: 6 -> 9, of which waited for: 5 -> 8; matrix products, arithmetic and copies ran while one was open for 5% -> 4% of each run, Pallas kernels for 0% -> 0%
where the time goes in v1:
time: 563 us; the launch traced here: 562 us
  waiting for transfers between devices  413 us (73%)
  starting transfers between devices  66.8 us (12%)
  local copies, waits for them, and re-layouts  34.6 us (6%)
  other arithmetic  31.5 us (6%)
  between operations  15.6 us (3%)
    ppermute x4, waiting for transfers between devices, body(): lax.ppermute(upstream, 'tile', [(dev, dev ^ hop) for dev in range(16)])  182 us
    psum x1, waiting for transfers between devices, spread(): return lax.psum(block, axis)  108 us
    all_gather x1, waiting for transfers between devices, body(): full_hidden = lax.all_gather(hidden_narrow, 'tile', axis=1, tiled=True)  91.3 us
    ppermute x1, starting transfers between devices, partner(): lax.ppermute(value, axis, [(i, i ^ 1 << distance) for i in range(lax.axis...  58.9 us
    ppermute x1, waiting for transfers between devices, partner(): lax.ppermute(value, axis, [(i, i ^ 1 << distance) for i in range(lax.axis...  29.6 us
    broadcast_in_dim x3, other arithmetic, body(): return (fields_next[None], out_next[None], hidden_next[None])  13.2 us
  transfers between devices with their start and end apart: 9, of which 8 were waited for; matrix products, arithmetic and copies ran while one was open for 4% of the time, Pallas kernels for 0%

profile of v1, /device:TPU:0, one launch (start us, length us, event | category | flops | bytes accessed | tf_op | source)
XLA Modules:
  0.0 562.2 jit_solution(3820966471867848347)
XLA Ops:
  8.1 2.4 bitcast_convert_fusion
  10.5 91.3 %all-gather.2.cloned.1.call-done = bf16[5,1024,1024]{2,1,0:T(8,128)(2,1)} async-done(((bf16[5,64,1024]{2,1,0:T(8,128)(2,1)}), bf16[5,1024,1024]{2,1,0:T(8,128)(2,1)}) %all-gather.2.cloned.1.call-update) | async-done | bytes 10485776 | tf_op jit(solution)/shard_map/all_gather | solution.py:72
  101.9 7.6 %conditional.4 = (f32[5,512,1024]{2,1,0:T(8,128)S(1)}, bf16[5,512,1024]{2,1,0:T(8,128)(2,1)}, f32[1024,1024]{1,0:T(8,128)}, f32[512,1024]{1,0:T(8,128)S(1)}, f32[1048576]{0:T(1024)S(1)}) conditional(s32[]{:T(128)} %convert_element_type.53, () %tuple.39, (bf16[5,1024,1024]{2,1,0:T(8,128)(2,1)}, bf16[512,1024]{1,0:T(8,128)(2,1)}, ...), branch_computations={%region_3.4_spmd, %region_4.5_spmd} | conditional | flops 8619819008 | bytes 199229664 | solution.py:38
  101.9 1.3 broadcast.47
  103.2 3.0 broadcast.48
  106.2 2.5 broadcast.49
  109.8 3.9 collective-permute-done.2
  114.7 47.2 %collective-permute-done.3 = f32[512,1024]{1,0:T(8,128)S(1)} collective-permute-done((f32[512,1024]{1,0:T(8,128)S(1)}, f32[512,1024]{1,0:T(8,128)S(1)}, u32[]{:S(2)}, u32[]{:S(2)}) %collective-permute-start.3) | collective-permute-done | bytes 2097184 | tf_op jit(solution)/shard_map/ppermute | solution.py:98
  163.1 46.2 %collective-permute-done.4 = f32[512,1024]{1,0:T(8,128)S(1)} collective-permute-done((f32[512,1024]{1,0:T(8,128)S(1)}, f32[512,1024]{1,0:T(8,128)S(1)}, u32[]{:S(2)}, u32[]{:S(2)}) %collective-permute-start.4) | collective-permute-done | bytes 2097184 | tf_op jit(solution)/shard_map/ppermute | solution.py:98
  209.9 1.6 collective-permute-start.5
  211.4 5.3 copy.14
  217.0 85.0 %collective-permute-done.5 = f32[512,1024]{1,0:T(8,128)} collective-permute-done((f32[512,1024]{1,0:T(8,128)S(1)}, f32[512,1024]{1,0:T(8,128)}, u32[]{:S(2)}, u32[]{:S(2)}) %collective-permute-start.5) | collective-permute-done | bytes 2097184 | tf_op jit(solution)/shard_map/ppermute | solution.py:98
  302.0 2.3 conditional.5
  302.0 1.2 broadcast.52
  304.3 6.5 %maximum_select_fusion = f32[1376256]{0:T(1024)} fusion(f32[327680]{0:T(1024)S(1)} %bitcast.250, f32[1048576]{0:T(1024)} %bitcast.242, f32[327680]{0:T(1024)} %get-tuple-element.72, f32[1048576]{0:T(1024)} %copy-done.3, pred[]{:T(512)S(6)} %eq.4), kind=kLoop, calls=%fused_computation.125 | loop fusion | flops 4128768 | bytes 16515073 | tf_op jit(solution)/shard_map/jit(_where)/select_n | solution.py:122
  310.8 58.9 %collective-permute-start.6 = (f32[1376256]{0:T(1024)}, f32[1376256]{0:T(1024)}, u32[]{:S(2)}, u32[]{:S(2)}) collective-permute-start(f32[1376256]{0:T(1024)} %maximum_select_fusion), channel_id=1, source_target_pairs={{0,16},{16,0},{1,17},{17,1},{2,18},{18,2},{3,19},{19,3},{4,20},{20... | collective-permute-start | bytes 16515080 | tf_op jit(solution)/shard_map/ppermute | solution.py:30
  369.9 4.4 collective-permute-start.1
  374.3 1.6 pad_maximum_fusion
  375.9 2.6 collective-permute-done
  378.5 3.1 concatenate.13
  381.6 3.2 conditional.3
  382.4 2.5 multiply_add_fusion.1
  384.9 3.2 broadcast_select_fusion
  388.7 107.6 %all-reduce.2.cloned.1.call-done = f32[512,1024]{1,0:T(8,128)} async-done(((f32[512,1024]{1,0:T(8,128)}), f32[512,1024]{1,0:T(8,128)}) %all-reduce.2.cloned.1.call-update) | async-done | bytes 2097168 | tf_op jit(solution)/shard_map/psum | solution.py:26
  496.3 4.4 gather_fusion
  500.7 3.2 select_bitcast_fusion.1
  503.9 29.6 %collective-permute-done.6 = f32[1376256]{0:T(1024)} collective-permute-done((f32[1376256]{0:T(1024)}, f32[1376256]{0:T(1024)}, u32[]{:S(2)}, u32[]{:S(2)}) %collective-permute-start.6) | collective-permute-done | bytes 5505056 | tf_op jit(solution)/shard_map/ppermute | solution.py:30
  533.5 1.4 slice.144
  535.1 4.4 slice.143
  539.6 5.1 slice.132
  544.7 3.0 fusion.100
  547.7 7.1 %select_bitcast_fusion = f32[1,1024,1024]{2,1,0:T(8,128)} fusion(f32[1024,1024]{1,0:T(8,128)} %get-tuple-element.73, f32[1024,1024]{1,0:T(8,128)} %slice.132, pred[]{:T(512)S(6)} %eq.4, f32[1,1024,1024]{2,1,0:T(8,128)S(1)} %copy-done), kind=kLoop, calls=%fused_computation.126 | loop fusion | flops 7340032 | bytes 16777216 | tf_op jit(solution)/shard_map/broadcast_in_dim | solution.py:138
  (43 shorter events, 6.9 us)
Async XLA Ops:
  8.0 93.9 %copy-start.8 = (f32[1,512,1024]{2,1,0:T(8,128)S(1)}, f32[1,512,1024]{2,1,0:T(8,128)}, u32[]{:S(2)}) copy-start(f32[1,512,1024]{2,1,0:T(8,128)} %param.13) | copy-start | bytes 6291460
  8.0 93.9 %all-gather.2.cloned.1.call-start = ((), (), s32[]{:S(2)}) async-start(), calls=%async_computation.1 | async-start | bytes 11141120 | tf_op jit(solution)/shard_map/all_gather | solution.py:72
  10.5 485.8 %all-reduce.2.cloned.1.call-start = ((), (), s32[]{:S(2)}) async-start(), calls=%async_computation | async-start | bytes 4194304 | tf_op jit(solution)/shard_map/psum | solution.py:26
  109.4 4.6 copy-start.3
  109.4 52.9 %copy-start.5 = (f32[5,512,1024]{2,1,0:T(8,128)}, f32[5,512,1024]{2,1,0:T(8,128)S(1)}, u32[]{:S(2)}) copy-start(f32[5,512,1024]{2,1,0:T(8,128)S(1)} %get-tuple-element.71) | copy-start | bytes 31457284
  109.5 4.2 collective-permute-start.2
  114.1 47.9 %collective-permute-start.3 = (f32[512,1024]{1,0:T(8,128)S(1)}, f32[512,1024]{1,0:T(8,128)S(1)}, u32[]{:S(2)}, u32[]{:S(2)}) collective-permute-start(f32[512,1024]{1,0:T(8,128)S(1)} %add.111), channel_id=1, source_target_pairs={{0,2},{1,3},{2,0},{3,1},{4,6},{5,7},{6,4},{7,5},{8,10},{9,11},{10,... | collective-permute-start | bytes 6291464 | tf_op jit(solution)/shard_map/ppermute | solution.py:98
  162.3 47.0 %collective-permute-start.4 = (f32[512,1024]{1,0:T(8,128)S(1)}, f32[512,1024]{1,0:T(8,128)S(1)}, u32[]{:S(2)}, u32[]{:S(2)}) collective-permute-start(f32[512,1024]{1,0:T(8,128)S(1)} %add.112), channel_id=1, source_target_pairs={{0,4},{1,5},{2,6},{3,7},{4,0},{5,1},{6,2},{7,3},{8,12},{9,13},{10,... | collective-permute-start | bytes 6291464 | tf_op jit(solution)/shard_map/ppermute | solution.py:98
  209.9 92.1 %collective-permute-start.5 = (f32[512,1024]{1,0:T(8,128)S(1)}, f32[512,1024]{1,0:T(8,128)}, u32[]{:S(2)}, u32[]{:S(2)}) collective-permute-start(f32[512,1024]{1,0:T(8,128)S(1)} %add.113), channel_id=1, source_target_pairs={{0,8},{1,9},{2,10},{3,11},{4,12},{5,13},{6,14},{7,15},{8,0},{9,1},... | collective-permute-start | bytes 6291464 | tf_op jit(solution)/shard_map/ppermute | solution.py:98
  211.4 5.3 copy-start.6
  304.3 65.4 %copy-start.9 = (f32[1,512,1024]{2,1,0:T(8,128)S(1)}, f32[1,512,1024]{2,1,0:T(8,128)}, u32[]{:S(2)}) copy-start(f32[1,512,1024]{2,1,0:T(8,128)} %param.13) | copy-start | bytes 6291460
  304.3 65.4 %copy-start.16 = (f32[1024]{0:T(1024)S(1)}, f32[1024]{0:T(1024)}, u32[]{:S(2)}) copy-start(f32[1024]{0:T(1024)} %param.14) | copy-start | bytes 12292
  310.8 222.8 %collective-permute-start.6 = (f32[1376256]{0:T(1024)}, f32[1376256]{0:T(1024)}, u32[]{:S(2)}, u32[]{:S(2)}) collective-permute-start(f32[1376256]{0:T(1024)} %maximum_select_fusion), channel_id=1, source_target_pairs={{0,16},{16,0},{1,17},{17,1},{2,18},{18,2},{3,19},{19,3},{4,20},{20... | collective-permute-start | bytes 16515080 | tf_op jit(solution)/shard_map/ppermute | solution.py:30
  369.8 8.7 %collective-permute-start = (f32[513,1]{1,0:T(8,128)S(1)}, f32[513,1]{1,0:T(8,128)S(1)}, u32[]{:S(2)}, u32[]{:S(2)}) collective-permute-start(f32[513,1]{1,0:T(8,128)S(1)} %get-tuple-element.97), channel_id=1, source_target_pairs={{0,1},{1,2},{2,3},{3,4},{4,5},{5,6},{6,7},{7,8},{8,9},{9,10},{10,1... | collective-permute-start | bytes 6164 | tf_op jit(solution)/shard_map/ppermute | solution.py:18
  369.9 8.6 %collective-permute-start.1 = (f32[513,1]{1,0:T(8,128)S(1)}, f32[513,1]{1,0:T(8,128)S(1)}, u32[]{:S(2)}, u32[]{:S(2)}) collective-permute-start(f32[513,1]{1,0:T(8,128)S(1)} %get-tuple-element.96), channel_id=1, source_target_pairs={{1,0},{2,1},{3,2},{4,3},{5,4},{6,5},{7,6},{8,7},{9,8},{10,9},{11,1... | collective-permute-start | bytes 6164 | tf_op jit(solution)/shard_map/ppermute | solution.py:19
  375.9 5.7 %copy-start.18 = (f32[1024]{0:T(1024)S(1)}, f32[1024]{0:T(1024)}, u32[]{:S(2)}) copy-start(f32[1024]{0:T(1024)} %param.15) | copy-start | bytes 12292
  388.0 0.7 copy-start.17
  539.6 5.1 copy-start.7
  544.7 3.0 copy-start
Sparse Core Ops, SparseCore 0:
  11.6 90.2 all-gather.1
Sparse Core Ops, SparseCore 1:
  388.1 108.1 all-reduce.1
